TPU v7x, 256 devices: a whole 4x4x8 slice. The times are simulated.
256 devices in a mesh: row: 16 (over z_lo, y, core), col: 16 (over z_hi, x).
Axes of the slice: x: 4, y: 4, z: 8 (z_hi: 4, z_lo: 2; z = z_hi * 2 + z_lo), core: 2. Of those that a mesh axis runs over, the one named last changes fastest.
Arguments:
- page_scores: bfloat16 [393216, 128], P('row'), may hold values from -6 to 6
- tile_values: bfloat16 [16, 16, 22, 512, 512], P('row', 'col'), may hold values from -0.25 to 0.25
- tile_row: int32 [16, 16, 22], P('row', 'col'), may hold values from 0 to 47, as said below
- tile_col: int32 [16, 16, 22], P('row', 'col'), may hold values from 0 to 7, as said below
- tile_count: int32 [16, 16], P('row', 'col'), may hold values from 2 to 22, as said below
- page_seed: int32 [393216], P(('row', 'col')), may hold values 0 or 1
- page_label: int32 [393216], P(('row', 'col')), may hold values from 0 to 127
- page_degree: int32 [393216], P(('row', 'col')), may hold values from 4 to 64
- feature_seed: int32 [65536], P('col'), may hold values 0 or 1
- feature_label: int32 [65536], P('col'), may hold values from 0 to 127
- feature_degree: int32 [65536], P('col'), may hold values from 4 to 64
Outputs:
- new_page_scores: bfloat16 [393216, 128], P(('row', 'col'))
Inputs may be any that keep to these rules, and one draw needn't show every extreme that they name: `tile_row`: within each grid cell the first tile_count slots name distinct tile positions; later slots are unused. `tile_col`: paired with tile_row slot by slot. `tile_count`: some grid cell has all 22 slots live in every draw.
All inputs are finite; a program needn't handle non-finite values. No bound on the sum of `page_seed` or of `feature_seed` on one device may be relied on, other than what follows from the above.
Results may differ from a plain program's by a relative error of at most 0.0047.
Values may be sent and summed in bfloat16 or wider, within the bound.
No kernel may reach another device: no remote copies, remote signals or barrier semaphores. Data moves between devices by JAX's collectives and lax.ppermute only.
A program may use at most 128 MiB of HBM per device.

v0:
```python
import jax
import jax.numpy as jnp
from jax import lax
from jax.sharding import PartitionSpec as P


def clamp_scores(sums, degree, known, label):
    classes = lax.broadcasted_iota(jnp.int32, sums.shape, 1)
    hot = (label[:, None] == classes).astype(jnp.float32)
    scaled = sums * lax.rsqrt(degree.astype(jnp.float32))[:, None]
    return jnp.where(known[:, None] == 1, hot, scaled)


def tile_products(tiles, src_index, dst_index, count, source, transposed, rows_out):
    edge = tiles.shape[-1]
    if transposed:
        dims = (((0,), (0,)), ((), ()))
    else:
        dims = (((1,), (0,)), ((), ()))

    def step(slot, total):
        tile = lax.dynamic_index_in_dim(tiles, slot, 0, keepdims=False)
        src = src_index[slot] * edge
        dst = dst_index[slot] * edge
        block = lax.dynamic_slice_in_dim(source, src, edge, 0)
        term = lax.dot_general(tile, block, dims, preferred_element_type=jnp.float32)
        old = lax.dynamic_slice_in_dim(total, dst, edge, 0)
        return lax.dynamic_update_slice_in_dim(total, old + term, dst, 0)

    start = jnp.zeros((rows_out, source.shape[1]), jnp.float32)
    return lax.fori_loop(0, count, step, start)


def local(
    page_scores,
    tile_values,
    tile_row,
    tile_col,
    tile_count,
    page_seed,
    page_label,
    page_degree,
    feature_seed,
    feature_label,
    feature_degree,
):
    tiles = tile_values[0, 0]
    rows_here = tile_row[0, 0]
    cols_here = tile_col[0, 0]
    count = tile_count[0, 0]
    feat_rows = feature_seed.shape[0]
    page_rows = page_scores.shape[0]
    partial_feat = tile_products(tiles, rows_here, cols_here, count, page_scores, True, feat_rows)
    summed = lax.psum(partial_feat, "row")
    feature_scores = clamp_scores(summed, feature_degree, feature_seed, feature_label).astype(
        jnp.bfloat16
    )
    partial_page = tile_products(
        tiles, cols_here, rows_here, count, feature_scores, False, page_rows
    )
    page_share = lax.psum_scatter(partial_page, "col", scatter_dimension=0, tiled=True)
    return clamp_scores(page_share, page_degree, page_seed, page_label).astype(jnp.bfloat16)


def solution(mesh):
    in_specs = (
        P("row", None),
        P("row", "col", None, None, None),
        P("row", "col", None),
        P("row", "col", None),
        P("row", "col"),
        P(("row", "col")),
        P(("row", "col")),
        P(("row", "col")),
        P("col"),
        P("col"),
        P("col"),
    )
    out_specs = P(("row", "col"), None)
    return jax.shard_map(local, mesh=mesh, in_specs=in_specs, out_specs=out_specs, check_vma=False)
```

profile of v0, /device:TPU:1, one launch (start us, length us, event | category | flops | bytes accessed | tf_op | source)
XLA Modules:
  0.0 566.8 jit_solution(10312019691434972564)
XLA Ops:
  6.5 0.0 all-reduce.2.cloned.1.call-start
  6.5 0.1 broadcast_in_dim.31
  6.7 24.5 %while.20 = (s32[]{:T(128)}, f32[4096,128]{1,0:T(8,128)S(1)}, s32[]{:T(128)}, s32[22]{0:T(128)}, bf16[22,512,512]{2,1,0:T(8,128)(2,1)}, /*index=5*/s32[22]{0:T(1...) while((s32[]{:T(128)}, f32[4096,128]{1,0:T(8,128)S(1)}, ...), condition=%wide.region_1.2_spmd, body=%wide.region_0.1_spmd.sunk | while | flops 67174416 | bytes 1179935 | solution.py:31
  7.4 1.3 dynamic_slice.59
  9.3 1.3 dynamic_slice.58
  11.2 1.4 fusion.18
  13.3 1.3 dynamic_slice.59
  15.3 1.3 dynamic_slice.58
  17.2 1.4 fusion.18
  19.3 1.3 dynamic_slice.59
  21.2 1.3 dynamic_slice.58
  23.2 1.4 fusion.18
  25.3 1.3 dynamic_slice.59
  27.2 1.3 dynamic_slice.58
  29.1 1.4 fusion.18
  31.2 0.0 copy-start
  31.2 1.3 copy-done
  32.5 0.0 all-reduce.2.cloned.1.call-update
  32.6 0.0 reduce-scatter.2.cloned.1.call-start
  32.6 0.0 copy-done.2
  32.7 238.2 %all-reduce.2.cloned.1.call-done = f32[4096,128]{1,0:T(8,128)} async-done(((f32[4096,128]{1,0:T(8,128)}), f32[4096,128]{1,0:T(8,128)}) %all-reduce.2.cloned.1.call-update) | async-done | bytes 2097168 | tf_op jit(solution)/shard_map/psum | solution.py:54
  270.9 5.9 %select_convert_fusion = bf16[4096,128]{1,0:T(8,128)(2,1)S(1)} fusion(f32[4096,128]{1,0:T(8,128)} %all-reduce.2.cloned.1.call-done, f32[4096]{0:T(1024)S(1)} %convert_rsqrt_fusion, s32[4096]{0:T(1024)S(1)} %copy-done.1, pred[4096]{0:T(1024)(128)(4,1)S(1)} %broadcast_compare_fusion), kind=kLoop, calls=%fused_computation.12 | loop fusion | flops 2621440 | bytes 3182592 | tf_op jit(solution)/shard_map/convert_element_type | solution.py:55
  276.8 0.0 copy-start.7
  276.8 0.0 copy-start.8
  276.8 4.8 broadcast_in_dim.29
  281.6 0.0 copy-done.8
  281.6 21.6 %while.21 = (s32[]{:T(128)}, f32[24576,128]{1,0:T(8,128)}, s32[]{:T(128)}, s32[22]{0:T(128)S(1)}, bf16[22,512,512]{2,1,0:T(8,128)(2,1)}, /*index=5*/s32[22]{0:T(...) while((s32[]{:T(128)}, f32[24576,128]{1,0:T(8,128)}, ...), condition=%wide.region_4.5_spmd, body=%wide.region_3.4_spmd.sunk | while | flops 67174416 | bytes 1179935 | solution.py:31
  282.3 0.6 dynamic_slice.64
  283.5 0.6 dynamic_slice.63
  284.8 2.1 fusion.21
  287.6 0.6 dynamic_slice.64
  288.8 0.6 dynamic_slice.63
  290.0 2.1 fusion.21
  292.8 0.6 dynamic_slice.64
  294.0 0.6 dynamic_slice.63
  295.2 2.1 fusion.21
  298.0 0.6 dynamic_slice.64
  299.2 0.6 dynamic_slice.63
  300.5 2.1 fusion.21
  303.3 0.0 copy-start.5
  303.3 0.0 copy-start.6
  303.3 0.0 copy-start.4
  303.3 0.0 reduce-scatter.2.cloned.1.call-update
  303.3 0.6 copy-done.5
  304.0 0.0 copy-done.6
  304.0 252.5 %reduce-scatter.2.cloned.1.call-done = f32[1536,128]{1,0:T(8,128)} async-done(((f32[24576,128]{1,0:T(8,128)}), f32[1536,128]{1,0:T(8,128)}) %reduce-scatter.2.cloned.1.call-update) | async-done | bytes 786448 | tf_op jit(solution)/shard_map/reduce_scatter | solution.py:61
  556.5 0.0 copy-done.4
  556.5 3.4 select_convert_fusion.1
  (10 shorter events, 0.0 us)
Async XLA Ops:
  6.5 26.1 %copy-start.2 = (s32[4096]{0:T(1024)S(1)}, s32[4096]{0:T(1024)}, u32[]{:S(2)}) copy-start(s32[4096]{0:T(1024)} %param.23) | copy-start | bytes 49156
  6.5 26.1 %copy-start.3 = (s32[4096]{0:T(1024)S(1)}, s32[4096]{0:T(1024)}, u32[]{:S(2)}) copy-start(s32[4096]{0:T(1024)} %param.25) | copy-start | bytes 49156
  6.5 264.3 %copy-start.1 = (s32[4096]{0:T(1024)S(1)}, s32[4096]{0:T(1024)}, u32[]{:S(2)}) copy-start(s32[4096]{0:T(1024)} %param.24) | copy-start | bytes 49156
  6.5 264.3 %all-reduce.2.cloned.1.call-start = ((), (), s32[]{:S(2)}) async-start(), calls=%async_computation.1 | async-start | bytes 4194304 | tf_op jit(solution)/shard_map/psum | solution.py:54
  31.2 1.3 copy-start
  32.6 523.9 %reduce-scatter.2.cloned.1.call-start = ((), (), s32[]{:S(2)}) async-start(), calls=%async_computation.2 | async-start | bytes 13369344 | tf_op jit(solution)/shard_map/reduce_scatter | solution.py:61
  276.8 4.8 copy-start.7
  276.8 4.8 copy-start.8
  303.3 0.7 copy-start.5
  303.3 0.7 copy-start.6
  303.3 253.2 %copy-start.4 = (s32[1536]{0:T(1024)S(1)}, s32[1536]{0:T(1024)}, u32[]{:S(2)}) copy-start(s32[1536]{0:T(1024)} %param.21) | copy-start | bytes 18436
Sparse Core Ops, SparseCore 0:
  32.7 238.1 all-reduce.1
  303.4 253.0 reduce-scatter.1
where the time goes:
time: 570 us; the launch traced here: 567 us
  waiting for transfers between devices  491 us (86%)
  local copies, waits for them, and re-layouts  22.1 us (4%)
  loops' own time  16.7 us (3%)
  matrix products  14.2 us (2%)
  between operations  13.5 us (2%)
  other arithmetic  9.4 us (2%)
    reduce_scatter x1, waiting for transfers between devices, local(): lax.psum_scatter(partial_page, 'col', scatter_dimension=0, tiled=True)  253 us
    psum x1, waiting for transfers between devices, local(): summed = lax.psum(partial_feat, 'row')  238 us
    another operation x2, loops' own time, tile_products(): return lax.fori_loop(0, count, step, start)  16.7 us
    dot_general x8, matrix products, step(): lax.dot_general(tile, block, dims, preferred_element_type=jnp.float32)  14.2 us
  transfers between devices with their start and end apart: 2, of which 2 were waited for; matrix products, arithmetic and copies ran while one was open for 0% of the time, Pallas kernels for 0%

commit v1 on v0

v1 whole, which is shorter than its diff:
```python
import functools

import jax
import jax.numpy as jnp
from jax import lax
from jax.experimental import pallas as pl
from jax.experimental.pallas import tpu as pltpu
from jax.sharding import Mesh, PartitionSpec as P

BF16 = jnp.bfloat16
F32 = jnp.float32
ROW = ("zlo", "y", "core")
COL = ("zhi", "x")
TILE_DOT = (((1,), (0,)), ((), ()))
TILE_T_DOT = (((0,), (0,)), ((), ()))


def clamp(sums, degree, known, label):
    classes = lax.broadcasted_iota(jnp.int32, sums.shape, 1)
    hot = (label[:, None] == classes).astype(F32)
    scaled = sums * lax.rsqrt(degree.astype(F32))[:, None]
    return jnp.where(known[:, None] == 1, hot, scaled).astype(BF16)


def add(*terms):
    total = terms[0].astype(F32)
    for term in terms[1:]:
        total = total + term.astype(F32)
    return total


def feature_kernel(row_ref, col_ref, count_ref, tiles, pages, out, tile_buf, page_buf, acc, sems):
    edge = tile_buf.shape[1]
    count = count_ref[0]

    def copies(slot):
        src = pl.multiple_of(row_ref[slot] * edge, edge)
        return (
            pltpu.make_async_copy(tiles.at[slot], tile_buf.at[slot], sems.at[0, slot]),
            pltpu.make_async_copy(pages.at[pl.ds(src, edge)], page_buf.at[slot], sems.at[1, slot]),
        )

    @pl.loop(0, count)
    def _(slot):
        for copy in copies(slot):
            copy.start()

    acc[...] = jnp.zeros_like(acc)

    @pl.loop(0, count)
    def _(slot):
        for copy in copies(slot):
            copy.wait()
        dst = pl.ds(pl.multiple_of(col_ref[slot] * edge, edge), edge)
        acc[dst, :] += lax.dot_general(
            tile_buf[slot], page_buf[slot], TILE_T_DOT, preferred_element_type=F32
        )

    out[...] = acc[...].astype(BF16)


def feature_partials(rows, cols, count, tiles, pages, feats):
    slots, edge, _ = tiles.shape
    classes = pages.shape[1]
    return pl.pallas_call(
        feature_kernel,
        out_shape=jax.ShapeDtypeStruct((feats, classes), BF16),
        in_specs=[pl.BlockSpec(memory_space=pltpu.SMEM)] * 3
        + [pl.BlockSpec(memory_space=pl.ANY)] * 2,
        out_specs=pl.BlockSpec(memory_space=pltpu.VMEM),
        scratch_shapes=[
            pltpu.VMEM((slots, edge, edge), BF16),
            pltpu.VMEM((slots, edge, classes), BF16),
            pltpu.VMEM((feats, classes), F32),
            pltpu.SemaphoreType.DMA((2, slots)),
        ],
        compiler_params=pltpu.CompilerParams(vmem_limit_bytes=32 << 20),
        cost_estimate=pl.CostEstimate(
            flops=2 * slots * edge * edge * classes,
            bytes_accessed=2 * slots * edge * (edge + classes),
            transcendentals=0,
        ),
        name="feature_partials",
    )(rows, cols, count, tiles, pages)


def page_kernel(deltas, per, row_ref, col_ref, count_ref, place, tiles, feats, *rest):
    n_out = 2 * len(deltas)
    outs, (tile_buf, acc, head, nxt, sems) = rest[:n_out], rest[n_out:]
    edge = tile_buf.shape[1]
    half = edge // 2
    page_tiles = head.shape[0]
    count = count_ref[0]

    @pl.loop(0, page_tiles)
    def _(r):
        head[r] = -1

    @pl.loop(0, count)
    def _(slot):
        r = row_ref[slot]
        nxt[slot] = head[r]
        head[r] = slot

    def copy(slot):
        return pltpu.make_async_copy(tiles.at[slot], tile_buf.at[slot], sems.at[slot])

    def page_tile(delta, index):
        ahead = index // per
        owner = lax.rem(place[1] + ahead, 4) * 4 + lax.rem(place[0] + delta, 4)
        return owner * per + lax.rem(index, per)

    for delta in deltas:

        @pl.loop(0, 4 * per)
        def _(index):
            def body(slot):
                copy(slot).start()
                return nxt[slot]

            lax.while_loop(lambda s: s >= 0, body, head[page_tile(delta, index)])

    for i, delta in enumerate(deltas):

        @pl.loop(0, 4 * per)
        def _(index):
            first = head[page_tile(delta, index)]

            @pl.when(first < 0)
            def _():
                outs[2 * i][index] = jnp.zeros((half, acc.shape[1]), BF16)
                outs[2 * i + 1][index] = jnp.zeros((half, acc.shape[1]), BF16)

            @pl.when(first >= 0)
            def _():
                def product(slot):
                    copy(slot).wait()
                    src = pl.ds(pl.multiple_of(col_ref[slot] * edge, edge), edge)
                    return lax.dot_general(
                        tile_buf[slot], feats[src, :], TILE_DOT, preferred_element_type=F32
                    )

                acc[...] = product(first)

                def body(slot):
                    acc[...] += product(slot)
                    return nxt[slot]

                lax.while_loop(lambda s: s >= 0, body, nxt[first])
                outs[2 * i][index] = acc[:half, :].astype(BF16)
                outs[2 * i + 1][index] = acc[half:, :].astype(BF16)


def page_partials(deltas, rows, cols, count, place, tiles, feats, page_tiles):
    slots, edge, _ = tiles.shape
    classes = feats.shape[1]
    per = page_tiles // 16
    piece = jax.ShapeDtypeStruct((4 * per, edge // 2, classes), BF16)
    out = pl.pallas_call(
        functools.partial(page_kernel, deltas, per),
        out_shape=[piece] * (2 * len(deltas)),
        in_specs=[pl.BlockSpec(memory_space=pltpu.SMEM)] * 4
        + [pl.BlockSpec(memory_space=pl.ANY), pl.BlockSpec(memory_space=pltpu.VMEM)],
        out_specs=[pl.BlockSpec(memory_space=pltpu.VMEM)] * (2 * len(deltas)),
        scratch_shapes=[
            pltpu.VMEM((slots, edge, edge), BF16),
            pltpu.VMEM((edge, classes), F32),
            pltpu.SMEM((page_tiles,), jnp.int32),
            pltpu.SMEM((slots,), jnp.int32),
            pltpu.SemaphoreType.DMA((slots,)),
        ],
        compiler_params=pltpu.CompilerParams(vmem_limit_bytes=32 << 20),
        cost_estimate=pl.CostEstimate(
            flops=2 * slots * edge * edge * classes * len(deltas) // 4,
            bytes_accessed=2 * slots * edge * edge * len(deltas) // 4,
            transcendentals=0,
        ),
        name="page_partials",
    )(rows, cols, count, place, tiles, feats)
    return [out[2 * i : 2 * i + 2] for i in range(len(deltas))]


def shift(x, axis, by):
    return lax.ppermute(x, axis, [(i, (i + by) % 4) for i in range(4)])


def ring_sums(pieces, axis):
    far_up = shift(pieces[2][0], axis, 1)
    far_down = shift(pieces[2][1], axis, 3)
    near_up = shift(pieces[1][1], axis, 1)
    near_down = shift(pieces[3][0], axis, 3)
    up = shift(add(far_up, pieces[1][0]).astype(BF16), axis, 1)
    down = shift(add(far_down, pieces[3][1]).astype(BF16), axis, 3)
    return add(pieces[0][0], near_down, up), add(pieces[0][1], near_up, down)


def local(
    page_scores,
    tile_values,
    tile_row,
    tile_col,
    tile_count,
    page_seed,
    page_label,
    page_degree,
    feature_seed,
    feature_label,
    feature_degree,
):
    tiles = tile_values[0, 0]
    rows, cols = tile_row[0, 0], tile_col[0, 0]
    count = tile_count[0]
    edge = tiles.shape[-1]
    feats, classes = feature_seed.shape[0], page_scores.shape[1]
    page_tiles = page_scores.shape[0] // edge
    share = feats // 16

    partial = feature_partials(rows, cols, count, tiles, page_scores, feats)
    parts = lax.all_to_all(partial.reshape(16, share, classes), ROW, 0, 0)
    mine = lax.axis_index(ROW) * share

    def own(x):
        return lax.dynamic_slice_in_dim(x, mine, share, 0)

    scores = clamp(
        parts.astype(F32).sum(0), own(feature_degree), own(feature_seed), own(feature_label)
    )
    feature_scores = lax.all_to_all(
        jnp.broadcast_to(scores[None], (16, share, classes)), ROW, 0, 0
    ).reshape(feats, classes)

    place = jnp.stack([lax.axis_index("x"), lax.axis_index("zhi")]).astype(jnp.int32)
    pieces = {}
    (pieces[2],) = page_partials(
        (2,), rows, cols, count, place, tiles, feature_scores, page_tiles
    )
    pieces[1], pieces[3], pieces[0] = page_partials(
        (1, 3, 0), rows, cols, count, place, tiles, feature_scores, page_tiles
    )
    first = ring_sums(pieces, "x")
    per = page_tiles // 16
    halves = [h.astype(BF16).reshape(4, per, edge // 2, classes) for h in first]
    top, bottom = ring_sums([[h[d] for h in halves] for d in range(4)], "zhi")
    sums = jnp.stack([top, bottom], 1).reshape(per * edge, classes)
    return clamp(sums, page_degree, page_seed, page_label)


def solution(mesh):
    parts = Mesh(mesh.devices.reshape(2, 4, 2, 4, 4), ROW + COL)
    in_specs = (
        P(ROW, None),
        P(ROW, COL, None, None, None),
        P(ROW, COL, None),
        P(ROW, COL, None),
        P(ROW, COL),
        P(ROW + COL),
        P(ROW + COL),
        P(ROW + COL),
        P(COL),
        P(COL),
        P(COL),
    )
    return jax.shard_map(
        local, mesh=parts, in_specs=in_specs, out_specs=P(ROW + COL, None), check_vma=False
    )
```

time: 570 us -> 160 us (0.28)
  the two profiles are of different devices: /device:TPU:1 before, /device:TPU:24 now
where the time goes in v1:
time: 160 us
  waiting for transfers between devices  80.7 us (50%)
  starting transfers between devices  43.6 us (27%)
  local copies, waits for them, and re-layouts  15.3 us (10%)
  Pallas kernels  13.6 us (8%)
  other arithmetic  5.52 us (3%)
    ppermute x12, waiting for transfers between devices, shift(): return lax.ppermute(x, axis, [(i, (i + by) % 4) for i in range(4)])  52.7 us
    ppermute x12, starting transfers between devices, shift(): return lax.ppermute(x, axis, [(i, (i + by) % 4) for i in range(4)])  26.9 us
    all_to_all x1, waiting for transfers between devices, local(): lax.all_to_all(jnp.broadcast_to(scores[None], (16, share, classes)), ROW,...  14.9 us
    unnamed x20, local copies, waits for them, and re-layouts  13.2 us
    all_to_all x1, waiting for transfers between devices, local(): parts = lax.all_to_all(partial.reshape(16, share, classes), ROW, 0, 0)  13.2 us
    all_to_all x1, starting transfers between devices, local(): parts = lax.all_to_all(partial.reshape(16, share, classes), ROW, 0, 0)  12 us
    pallas_call x2, Pallas kernels, page_partials(): pl.pallas_call(functools.partial(page_kernel, deltas, per), out_shape=[pi...  7.95 us
    pallas_call x1, Pallas kernels, feature_partials(): pl.pallas_call(feature_kernel, out_shape=jax.ShapeDtypeStruct((feats, cla...  5.61 us
  transfers between devices with their start and end apart: 14, of which 8 were waited for; matrix products, arithmetic and copies ran while one was open for 2% of the time, Pallas kernels for 3%

profile of v1, /device:TPU:24, one launch (start us, length us, event | category | flops | bytes accessed | tf_op | source)
XLA Modules:
  0.0 159.6 jit_solution(9566480815450792282)
XLA Ops:
  0.7 0.0 copy-start
  0.7 4.3 %copy-done = bf16[1,1,22,512,512]{4,3,2,1,0:T(8,128)(2,1)S(1)} copy-done((bf16[1,1,22,512,512]{4,3,2,1,0:T(8,128)(2,1)S(1)}, bf16[1,1,22,512,512]{4,3,2,1,0:T(8,128)(2,1)}, u32[]{:S(2)}) %copy-start) | copy-done | bytes 11534360
  4.9 2.8 %copy-done.2 = bf16[24576,128]{1,0:T(8,128)(2,1)S(1)} copy-done((bf16[24576,128]{1,0:T(8,128)(2,1)S(1)}, bf16[24576,128]{1,0:T(8,128)(2,1)}, u32[]{:S(2)}) %copy-start.2) | copy-done | bytes 6291480
  7.7 0.7 copy-done.3
  8.4 0.7 copy-done.5
  9.0 5.6 %feature_partials.1 = bf16[4096,128]{1,0:T(8,128)(2,1)} custom-call(s32[22]{0:T(128)S(1)} %bitcast.26, s32[22]{0:T(128)S(1)} %bitcast.29, s32[1]{0:T(128)} %bitcast.18.count_ref, bf16[22,512,512]{2,1,0:T(8,128)(2,1)S(1)} %bitcast.21, bf16[24576,128]{1,0:T(8,128)(2,1)S(1)} %copy-done.2), custom_call_target="tpu_custom_call" | custom-call | flops 1476395008 | bytes 14417920 | tf_op jit(solution)/shard_map/feature_partials/pallas_call | solution.py:65
  14.6 12.0 %all-to-all-start = ((bf16[16,256,128]{2,1,0:T(8,128)(2,1)}), bf16[16,256,128]{2,1,0:T(8,128)(2,1)S(1)}, u32[]{:S(2)}, u32[]{:S(2)}) async-start(bf16[16,256,128]{2,1,0:T(8,128)(2,1)} %bitcast.6), calls=%async_computation | async-start | bytes 2097152 | tf_op jit(solution)/shard_map/all_to_all | solution.py:219
  26.7 0.8 dynamic_slice.10
  27.4 0.8 dynamic-slice_compare_fusion
  28.2 0.8 convert_rsqrt_fusion.1
  29.0 13.2 %all-to-all-done = bf16[16,256,128]{2,1,0:T(8,128)(2,1)S(1)} async-done(((bf16[16,256,128]{2,1,0:T(8,128)(2,1)}), bf16[16,256,128]{2,1,0:T(8,128)(2,1)S(1)}, u32[]{:S(2)}, u32[]{:S(2)}) %all-to-all-start) | async-done | bytes 1048608 | tf_op jit(solution)/shard_map/all_to_all | solution.py:219
  42.1 0.1 convert_reduce_fusion
  42.3 0.2 select_convert_fusion
  42.5 1.2 broadcast_in_dim.17
  43.7 4.7 %all-to-all-start.1 = ((bf16[16,256,128]{2,1,0:T(8,128)(2,1)}), bf16[16,256,128]{2,1,0:T(8,128)(2,1)S(1)}, u32[]{:S(2)}, u32[]{:S(2)}) async-start(bf16[16,256,128]{2,1,0:T(8,128)(2,1)} %broadcast_in_dim.17), calls=%async_computation.1 | async-start | bytes 2097152 | tf_op jit(solution)/shard_map/all_to_all | solution.py:228
  48.4 0.1 pad_add_fusion.place
  48.5 14.9 %all-to-all-done.1 = bf16[16,256,128]{2,1,0:T(8,128)(2,1)S(1)} async-done(((bf16[16,256,128]{2,1,0:T(8,128)(2,1)}), bf16[16,256,128]{2,1,0:T(8,128)(2,1)S(1)}, u32[]{:S(2)}, u32[]{:S(2)}) %all-to-all-start.1) | async-done | bytes 1048608 | tf_op jit(solution)/shard_map/all_to_all | solution.py:228
  63.3 4.3 %copy-done.1 = bf16[1,1,22,512,512]{4,3,2,1,0:T(8,128)(2,1)S(1)} copy-done((bf16[1,1,22,512,512]{4,3,2,1,0:T(8,128)(2,1)S(1)}, bf16[1,1,22,512,512]{4,3,2,1,0:T(8,128)(2,1)}, u32[]{:S(2)}) %copy-start.1) | copy-done | bytes 11534360
  67.6 2.4 %page_partials.3 = (bf16[12,256,128]{2,1,0:T(8,128)(2,1)S(1)}, bf16[12,256,128]{2,1,0:T(8,128)(2,1)S(1)}) custom-call(s32[22]{0:T(128)S(1)} %bitcast.27, s32[22]{0:T(128)S(1)} %bitcast.30, s32[1]{0:T(128)} %bitcast.20.count_ref, s32[2]{0:T(128)S(1)} %pad_add_fusion.place, bf16[22,512,512]{2,1,0:T(8,128)(2,1)S(1)} %bitcast.22, bf16[4096,128]{1,0:T(8,128)(2,1)S(1)} %bitcast.24), custom_call_target="tpu_custom_call" | custom-call | flops 369098752 | bytes 2883584 | tf_op jit(solution)/shard_map/page_partials/pallas_call | solution.py:159
  70.0 5.7 %collective-permute-start.1 = (bf16[12,256,128]{2,1,0:T(8,128)(2,1)S(1)}, bf16[12,256,128]{2,1,0:T(8,128)(2,1)S(1)}, u32[]{:S(2)}, u32[]{:S(2)}) collective-permute-start(bf16[12,256,128]{2,1,0:T(8,128)(2,1)S(1)} %get-tuple-element.15), channel_id=1, source_target_pairs={{0,1},{1,2},{2,3},{3,0},{4,5},{5,6},{6,7},{7,4},{8,9},{9,10},{10,1... | collective-permute-start | bytes 2359304 | tf_op jit(solution)/shard_map/ppermute | solution.py:184
  75.7 5.6 %page_partials.2 = (bf16[12,256,128]{2,1,0:T(8,128)(2,1)S(1)}, bf16[12,256,128]{2,1,0:T(8,128)(2,1)S(1)}, bf16[12,256,128]{2,1,0:T(8,128)(2,1)S(1)}, bf16[12,256...) custom-call(s32[22]{0:T(128)S(1)} %bitcast.28, s32[22]{0:T(128)S(1)} %bitcast.31, ...), custom_call_target="tpu_custom_call" | custom-call | flops 1107296256 | bytes 8650752 | tf_op jit(solution)/shard_map/page_partials/pallas_call | solution.py:159
  81.3 0.9 collective-permute-start
  82.1 11.4 %collective-permute-done.1 = bf16[12,256,128]{2,1,0:T(8,128)(2,1)S(1)} collective-permute-done((bf16[12,256,128]{2,1,0:T(8,128)(2,1)S(1)}, bf16[12,256,128]{2,1,0:T(8,128)(2,1)S(1)}, u32[]{:S(2)}, u32[]{:S(2)}) %collective-permute-start.1) | collective-permute-done | bytes 786464 | tf_op jit(solution)/shard_map/ppermute | solution.py:184
  93.5 0.3 add_convert_fusion.3
  93.8 2.0 %collective-permute-start.2 = (bf16[12,256,128]{2,1,0:T(8,128)(2,1)S(1)}, bf16[12,256,128]{2,1,0:T(8,128)(2,1)S(1)}, u32[]{:S(2)}, u32[]{:S(2)}) collective-permute-start(bf16[12,256,128]{2,1,0:T(8,128)(2,1)S(1)} %add_convert_fusion.3), channel_id=1, source_target_pairs={{0,1},{1,2},{2,3},{3,0},{4,5},{5,6},{6,7},{7,4},{8,9},{9,10},{10,1... | collective-permute-start | bytes 2359304 | tf_op jit(solution)/shard_map/ppermute | solution.py:184
  95.8 0.3 collective-permute-start.6
  96.1 0.2 add_convert_fusion.1
  96.4 3.0 %collective-permute-start.8 = (bf16[12,256,128]{2,1,0:T(8,128)(2,1)S(1)}, bf16[12,256,128]{2,1,0:T(8,128)(2,1)S(1)}, u32[]{:S(2)}, u32[]{:S(2)}) collective-permute-start(bf16[12,256,128]{2,1,0:T(8,128)(2,1)S(1)} %add_convert_fusion.1), channel_id=1, source_target_pairs={{0,3},{1,0},{2,1},{3,2},{4,7},{5,4},{6,5},{7,6},{8,11},{9,8},{10,9... | collective-permute-start | bytes 2359304 | tf_op jit(solution)/shard_map/ppermute | solution.py:184
  99.4 13.5 %collective-permute-done = bf16[12,256,128]{2,1,0:T(8,128)(2,1)S(1)} collective-permute-done((bf16[12,256,128]{2,1,0:T(8,128)(2,1)S(1)}, bf16[12,256,128]{2,1,0:T(8,128)(2,1)S(1)}, u32[]{:S(2)}, u32[]{:S(2)}) %collective-permute-start) | collective-permute-done | bytes 786464 | tf_op jit(solution)/shard_map/ppermute | solution.py:184
  112.9 2.6 %collective-permute-done.2 = bf16[12,256,128]{2,1,0:T(8,128)(2,1)S(1)} collective-permute-done((bf16[12,256,128]{2,1,0:T(8,128)(2,1)S(1)}, bf16[12,256,128]{2,1,0:T(8,128)(2,1)S(1)}, u32[]{:S(2)}, u32[]{:S(2)}) %collective-permute-start.2) | collective-permute-done | bytes 786464 | tf_op jit(solution)/shard_map/ppermute | solution.py:184
  115.5 0.3 add_convert_fusion.2
  115.9 2.7 %collective-permute-start.4 = (bf16[3,256,128]{2,1,0:T(8,128)(2,1)S(1)}, bf16[3,256,128]{2,1,0:T(8,128)(2,1)S(1)}, u32[]{:S(2)}, u32[]{:S(2)}) collective-permute-start(bf16[3,256,128]{2,1,0:T(8,128)(2,1)S(1)} %get-tuple-element.22), channel_id=1, source_target_pairs={{0,4},{4,8},{8,12},{12,0},{1,5},{5,9},{9,13},{13,1},{2,6},{6,10},{... | collective-permute-start | bytes 589832 | tf_op jit(solution)/shard_map/ppermute | solution.py:184
  118.5 2.6 %collective-permute-start.3 = (bf16[3,256,128]{2,1,0:T(8,128)(2,1)S(1)}, bf16[3,256,128]{2,1,0:T(8,128)(2,1)S(1)}, u32[]{:S(2)}, u32[]{:S(2)}) collective-permute-start(bf16[3,256,128]{2,1,0:T(8,128)(2,1)S(1)} %get-tuple-element.21), channel_id=1, source_target_pairs={{0,12},{4,0},{8,4},{12,8},{1,13},{5,1},{9,5},{13,9},{2,14},{6,2},{... | collective-permute-start | bytes 589832 | tf_op jit(solution)/shard_map/ppermute | solution.py:184
  121.1 10.5 %collective-permute-done.6 = bf16[12,256,128]{2,1,0:T(8,128)(2,1)S(1)} collective-permute-done((bf16[12,256,128]{2,1,0:T(8,128)(2,1)S(1)}, bf16[12,256,128]{2,1,0:T(8,128)(2,1)S(1)}, u32[]{:S(2)}, u32[]{:S(2)}) %collective-permute-start.6) | collective-permute-done | bytes 786464 | tf_op jit(solution)/shard_map/ppermute | solution.py:184
  131.6 0.3 add_convert_fusion
  131.9 4.4 %collective-permute-start.10 = (bf16[3,256,128]{2,1,0:T(8,128)(2,1)S(1)}, bf16[3,256,128]{2,1,0:T(8,128)(2,1)S(1)}, u32[]{:S(2)}, u32[]{:S(2)}) collective-permute-start(bf16[3,256,128]{2,1,0:T(8,128)(2,1)S(1)} %get-tuple-element.24), channel_id=1, source_target_pairs={{0,12},{4,0},{8,4},{12,8},{1,13},{5,1},{9,5},{13,9},{2,14},{6,2},{... | collective-permute-start | bytes 589832 | tf_op jit(solution)/shard_map/ppermute | solution.py:184
  136.3 0.1 add_convert_fusion.5
  136.4 2.2 %collective-permute-start.5 = (bf16[3,256,128]{2,1,0:T(8,128)(2,1)S(1)}, bf16[3,256,128]{2,1,0:T(8,128)(2,1)S(1)}, u32[]{:S(2)}, u32[]{:S(2)}) collective-permute-start(bf16[3,256,128]{2,1,0:T(8,128)(2,1)S(1)} %add_convert_fusion.5), channel_id=1, source_target_pairs={{0,4},{4,8},{8,12},{12,0},{1,5},{5,9},{9,13},{13,1},{2,6},{6,10},{... | collective-permute-start | bytes 589832 | tf_op jit(solution)/shard_map/ppermute | solution.py:184
  138.5 2.7 %collective-permute-done.10 = bf16[3,256,128]{2,1,0:T(8,128)(2,1)S(1)} collective-permute-done((bf16[3,256,128]{2,1,0:T(8,128)(2,1)S(1)}, bf16[3,256,128]{2,1,0:T(8,128)(2,1)S(1)}, u32[]{:S(2)}, u32[]{:S(2)}) %collective-permute-start.10) | collective-permute-done | bytes 196640 | tf_op jit(solution)/shard_map/ppermute | solution.py:184
  141.3 0.1 add_convert_fusion.4
  141.3 3.2 %collective-permute-start.11 = (bf16[3,256,128]{2,1,0:T(8,128)(2,1)S(1)}, bf16[3,256,128]{2,1,0:T(8,128)(2,1)S(1)}, u32[]{:S(2)}, u32[]{:S(2)}) collective-permute-start(bf16[3,256,128]{2,1,0:T(8,128)(2,1)S(1)} %add_convert_fusion.4), channel_id=1, source_target_pairs={{0,12},{4,0},{8,4},{12,8},{1,13},{5,1},{9,5},{13,9},{2,14},{6,2},{... | collective-permute-start | bytes 589832 | tf_op jit(solution)/shard_map/ppermute | solution.py:184
  144.5 12.0 %collective-permute-done.5 = bf16[3,256,128]{2,1,0:T(8,128)(2,1)S(1)} collective-permute-done((bf16[3,256,128]{2,1,0:T(8,128)(2,1)S(1)}, bf16[3,256,128]{2,1,0:T(8,128)(2,1)S(1)}, u32[]{:S(2)}, u32[]{:S(2)}) %collective-permute-start.5) | collective-permute-done | bytes 196640 | tf_op jit(solution)/shard_map/ppermute | solution.py:184
  156.5 0.1 add_bitcast_fusion.1
  156.6 0.1 add_bitcast_fusion
  156.7 0.1 pad_maximum_fusion
  156.8 0.1 copy.12
  156.8 0.6 copy-done.7
  157.4 2.2 %fusion.1 = bf16[1536,128]{1,0:T(8,128)(2,1)} fusion(f32[3,2,256,128]{3,2,1,0:T(8,128)S(1)} %copy.12, f32[1536]{0:T(1024)S(1)} %convert_rsqrt_fusion, s32[1536]{0:T(1024)S(1)} %copy-done.7, pred[1536]{0:T(1024)(128)(4,1)S(1)} %broadcast_compare_fusion), kind=kLoop, calls=%fused_computation.8 | loop fusion | flops 983040 | bytes 1193472 | tf_op jit(solution)/shard_map/convert_element_type | solution.py:22
  (25 shorter events, 0.1 us)
Async XLA Ops:
  0.7 4.3 %copy-start = (bf16[1,1,22,512,512]{4,3,2,1,0:T(8,128)(2,1)S(1)}, bf16[1,1,22,512,512]{4,3,2,1,0:T(8,128)(2,1)}, u32[]{:S(2)}) copy-start(bf16[1,1,22,512,512]{4,3,2,1,0:T(8,128)(2,1)} %param.12) | copy-start | bytes 34603012
  4.9 2.8 %copy-start.2 = (bf16[24576,128]{1,0:T(8,128)(2,1)S(1)}, bf16[24576,128]{1,0:T(8,128)(2,1)}, u32[]{:S(2)}) copy-start(bf16[24576,128]{1,0:T(8,128)(2,1)} %pages.1) | copy-start | bytes 18874372
  7.7 0.7 copy-start.3
  8.4 0.7 copy-start.5
  14.6 27.5 %all-to-all-start = ((bf16[16,256,128]{2,1,0:T(8,128)(2,1)}), bf16[16,256,128]{2,1,0:T(8,128)(2,1)S(1)}, u32[]{:S(2)}, u32[]{:S(2)}) async-start(bf16[16,256,128]{2,1,0:T(8,128)(2,1)} %bitcast.6), calls=%async_computation | async-start | bytes 2097152 | tf_op jit(solution)/shard_map/all_to_all | solution.py:219
  42.4 20.9 %copy-start.4 = (s32[1,1,22]{2,1,0:T(1,128)S(1)}, s32[1,1,22]{2,1,0:T(1,128)}, u32[]{:S(2)}) copy-start(s32[1,1,22]{2,1,0:T(1,128)} %param.13) | copy-start | bytes 268
  42.5 20.9 %copy-start.6 = (s32[1,1,22]{2,1,0:T(1,128)S(1)}, s32[1,1,22]{2,1,0:T(1,128)}, u32[]{:S(2)}) copy-start(s32[1,1,22]{2,1,0:T(1,128)} %param.14) | copy-start | bytes 268
  43.7 19.6 %all-to-all-start.1 = ((bf16[16,256,128]{2,1,0:T(8,128)(2,1)}), bf16[16,256,128]{2,1,0:T(8,128)(2,1)S(1)}, u32[]{:S(2)}, u32[]{:S(2)}) async-start(bf16[16,256,128]{2,1,0:T(8,128)(2,1)} %broadcast_in_dim.17), calls=%async_computation.1 | async-start | bytes 2097152 | tf_op jit(solution)/shard_map/all_to_all | solution.py:228
  63.3 4.3 %copy-start.1 = (bf16[1,1,22,512,512]{4,3,2,1,0:T(8,128)(2,1)S(1)}, bf16[1,1,22,512,512]{4,3,2,1,0:T(8,128)(2,1)}, u32[]{:S(2)}) copy-start(bf16[1,1,22,512,512]{4,3,2,1,0:T(8,128)(2,1)} %param.12) | copy-start | bytes 34603012
  70.0 23.5 %collective-permute-start.1 = (bf16[12,256,128]{2,1,0:T(8,128)(2,1)S(1)}, bf16[12,256,128]{2,1,0:T(8,128)(2,1)S(1)}, u32[]{:S(2)}, u32[]{:S(2)}) collective-permute-start(bf16[12,256,128]{2,1,0:T(8,128)(2,1)S(1)} %get-tuple-element.15), channel_id=1, source_target_pairs={{0,1},{1,2},{2,3},{3,0},{4,5},{5,6},{6,7},{7,4},{8,9},{9,10},{10,1... | collective-permute-start | bytes 2359304 | tf_op jit(solution)/shard_map/ppermute | solution.py:184
  75.7 20.5 %collective-permute-start.7 = (bf16[12,256,128]{2,1,0:T(8,128)(2,1)S(1)}, bf16[12,256,128]{2,1,0:T(8,128)(2,1)S(1)}, u32[]{:S(2)}, u32[]{:S(2)}) collective-permute-start(bf16[12,256,128]{2,1,0:T(8,128)(2,1)S(1)} %get-tuple-element.19), channel_id=1, source_target_pairs={{0,3},{1,0},{2,1},{3,2},{4,7},{5,4},{6,5},{7,6},{8,11},{9,8},{10,9... | collective-permute-start | bytes 2359304 | tf_op jit(solution)/shard_map/ppermute | solution.py:184
  81.3 31.7 %collective-permute-start = (bf16[12,256,128]{2,1,0:T(8,128)(2,1)S(1)}, bf16[12,256,128]{2,1,0:T(8,128)(2,1)S(1)}, u32[]{:S(2)}, u32[]{:S(2)}) collective-permute-start(bf16[12,256,128]{2,1,0:T(8,128)(2,1)S(1)} %get-tuple-element.14), channel_id=1, source_target_pairs={{0,3},{1,0},{2,1},{3,2},{4,7},{5,4},{6,5},{7,6},{8,11},{9,8},{10,9... | collective-permute-start | bytes 2359304 | tf_op jit(solution)/shard_map/ppermute | solution.py:184
  93.8 5.6 %copy-start.8 = (s32[1536]{0:T(1024)S(1)}, s32[1536]{0:T(1024)}, u32[]{:S(2)}) copy-start(s32[1536]{0:T(1024)} %param.16) | copy-start | bytes 18436
  93.8 5.6 %copy-start.9 = (s32[1536]{0:T(1024)S(1)}, s32[1536]{0:T(1024)}, u32[]{:S(2)}) copy-start(s32[1536]{0:T(1024)} %param.18) | copy-start | bytes 18436
  93.8 21.7 %collective-permute-start.2 = (bf16[12,256,128]{2,1,0:T(8,128)(2,1)S(1)}, bf16[12,256,128]{2,1,0:T(8,128)(2,1)S(1)}, u32[]{:S(2)}, u32[]{:S(2)}) collective-permute-start(bf16[12,256,128]{2,1,0:T(8,128)(2,1)S(1)} %add_convert_fusion.3), channel_id=1, source_target_pairs={{0,1},{1,2},{2,3},{3,0},{4,5},{5,6},{6,7},{7,4},{8,9},{9,10},{10,1... | collective-permute-start | bytes 2359304 | tf_op jit(solution)/shard_map/ppermute | solution.py:184
  95.8 35.7 %collective-permute-start.6 = (bf16[12,256,128]{2,1,0:T(8,128)(2,1)S(1)}, bf16[12,256,128]{2,1,0:T(8,128)(2,1)S(1)}, u32[]{:S(2)}, u32[]{:S(2)}) collective-permute-start(bf16[12,256,128]{2,1,0:T(8,128)(2,1)S(1)} %get-tuple-element.18), channel_id=1, source_target_pairs={{0,1},{1,2},{2,3},{3,0},{4,5},{5,6},{6,7},{7,4},{8,9},{9,10},{10,1... | collective-permute-start | bytes 2359304 | tf_op jit(solution)/shard_map/ppermute | solution.py:184
  96.4 35.2 %collective-permute-start.8 = (bf16[12,256,128]{2,1,0:T(8,128)(2,1)S(1)}, bf16[12,256,128]{2,1,0:T(8,128)(2,1)S(1)}, u32[]{:S(2)}, u32[]{:S(2)}) collective-permute-start(bf16[12,256,128]{2,1,0:T(8,128)(2,1)S(1)} %add_convert_fusion.1), channel_id=1, source_target_pairs={{0,3},{1,0},{2,1},{3,2},{4,7},{5,4},{6,5},{7,6},{8,11},{9,8},{10,9... | collective-permute-start | bytes 2359304 | tf_op jit(solution)/shard_map/ppermute | solution.py:184
  115.9 20.5 %collective-permute-start.4 = (bf16[3,256,128]{2,1,0:T(8,128)(2,1)S(1)}, bf16[3,256,128]{2,1,0:T(8,128)(2,1)S(1)}, u32[]{:S(2)}, u32[]{:S(2)}) collective-permute-start(bf16[3,256,128]{2,1,0:T(8,128)(2,1)S(1)} %get-tuple-element.22), channel_id=1, source_target_pairs={{0,4},{4,8},{8,12},{12,0},{1,5},{5,9},{9,13},{13,1},{2,6},{6,10},{... | collective-permute-start | bytes 589832 | tf_op jit(solution)/shard_map/ppermute | solution.py:184
  118.5 26.0 %collective-permute-start.3 = (bf16[3,256,128]{2,1,0:T(8,128)(2,1)S(1)}, bf16[3,256,128]{2,1,0:T(8,128)(2,1)S(1)}, u32[]{:S(2)}, u32[]{:S(2)}) collective-permute-start(bf16[3,256,128]{2,1,0:T(8,128)(2,1)S(1)} %get-tuple-element.21), channel_id=1, source_target_pairs={{0,12},{4,0},{8,4},{12,8},{1,13},{5,1},{9,5},{13,9},{2,14},{6,2},{... | collective-permute-start | bytes 589832 | tf_op jit(solution)/shard_map/ppermute | solution.py:184
  131.9 9.3 %collective-permute-start.10 = (bf16[3,256,128]{2,1,0:T(8,128)(2,1)S(1)}, bf16[3,256,128]{2,1,0:T(8,128)(2,1)S(1)}, u32[]{:S(2)}, u32[]{:S(2)}) collective-permute-start(bf16[3,256,128]{2,1,0:T(8,128)(2,1)S(1)} %get-tuple-element.24), channel_id=1, source_target_pairs={{0,12},{4,0},{8,4},{12,8},{1,13},{5,1},{9,5},{13,9},{2,14},{6,2},{... | collective-permute-start | bytes 589832 | tf_op jit(solution)/shard_map/ppermute | solution.py:184
  136.3 20.3 %collective-permute-start.9 = (bf16[3,256,128]{2,1,0:T(8,128)(2,1)S(1)}, bf16[3,256,128]{2,1,0:T(8,128)(2,1)S(1)}, u32[]{:S(2)}, u32[]{:S(2)}) collective-permute-start(bf16[3,256,128]{2,1,0:T(8,128)(2,1)S(1)} %get-tuple-element.23), channel_id=1, source_target_pairs={{0,4},{4,8},{8,12},{12,0},{1,5},{5,9},{9,13},{13,1},{2,6},{6,10},{... | collective-permute-start | bytes 589832 | tf_op jit(solution)/shard_map/ppermute | solution.py:184
  136.4 20.1 %collective-permute-start.5 = (bf16[3,256,128]{2,1,0:T(8,128)(2,1)S(1)}, bf16[3,256,128]{2,1,0:T(8,128)(2,1)S(1)}, u32[]{:S(2)}, u32[]{:S(2)}) collective-permute-start(bf16[3,256,128]{2,1,0:T(8,128)(2,1)S(1)} %add_convert_fusion.5), channel_id=1, source_target_pairs={{0,4},{4,8},{8,12},{12,0},{1,5},{5,9},{9,13},{13,1},{2,6},{6,10},{... | collective-permute-start | bytes 589832 | tf_op jit(solution)/shard_map/ppermute | solution.py:184
  141.3 15.3 %collective-permute-start.11 = (bf16[3,256,128]{2,1,0:T(8,128)(2,1)S(1)}, bf16[3,256,128]{2,1,0:T(8,128)(2,1)S(1)}, u32[]{:S(2)}, u32[]{:S(2)}) collective-permute-start(bf16[3,256,128]{2,1,0:T(8,128)(2,1)S(1)} %add_convert_fusion.4), channel_id=1, source_target_pairs={{0,12},{4,0},{8,4},{12,8},{1,13},{5,1},{9,5},{13,9},{2,14},{6,2},{... | collective-permute-start | bytes 589832 | tf_op jit(solution)/shard_map/ppermute | solution.py:184
  156.7 0.7 copy-start.7
